TPU v7x, 512 devices: a whole 4x8x8 slice. The times are simulated.
512 devices in a mesh: ctx: 16 (over y, core), head: 32 (over z, x).
Axes of the slice: x: 4, y: 8, z: 8, core: 2. Of those that a mesh axis runs over, the one named last changes fastest.
Arguments:
- query_rows: bfloat16 [6144, 64, 128], P('ctx', 'head'), may hold values from -1.75 to 1.75
- key_matrix: bfloat16 [6144, 64, 128], P('ctx', 'head'), may hold values from -1.75 to 1.75
- value_rows: bfloat16 [6144, 64, 128], P('ctx', 'head'), may hold values from -55 to 55
- decay_log: float32 [6144, 64], P('ctx', 'head'), may hold values from -0.6 to 0
- norm_gain: float32 [64, 128], P('head'), may hold values from 0.1 to 1.9
- grad_out: bfloat16 [6144, 64, 128], P('ctx', 'head'), may hold values from -6 to 6
Outputs:
- output: bfloat16 [6144, 64, 128], P('ctx', 'head')
- grad_query: bfloat16 [6144, 64, 128], P('ctx', 'head')
- grad_key: bfloat16 [6144, 64, 128], P('ctx', 'head')
- grad_value: bfloat16 [6144, 64, 128], P('ctx', 'head')
All inputs are finite; a program needn't handle non-finite values.
Results may differ from a plain program's by a relative error of at most 0.019.
Values sent between devices are 32-bit elements; how exact they have to be, the bound alone decides.
A program may use at most 64 MiB of HBM per device.

v0:
```python
import jax
import jax.numpy as jnp
from jax import lax
from jax.sharding import PartitionSpec as P

GROUP = 128


epsilon = 1e-06


def weigh_gathered(gathered, log_rates, position, forward):
    device_ranks = jnp.arange(log_rates.shape[0], dtype=jnp.int32)
    running = jnp.cumsum(log_rates, axis=0)
    own_total = running[position]
    if forward:
        keep_mask = device_ranks < position
        spread = (own_total - log_rates[position])[None, :] - running
    else:
        keep_mask = device_ranks > position
        spread = running - log_rates - own_total[None, :]
    keep_mask = keep_mask[:, None]
    factors = jnp.where(keep_mask, jnp.exp(jnp.where(keep_mask, spread, 0.0)), 0.0)
    return jnp.einsum("nh,nhde->hde", factors, gathered, precision=lax.Precision.HIGHEST)


def per_device(query_rows, key_matrix, value_rows, decay_log, norm_gain, grad_out):
    token_count, head_count, head_size = query_rows.shape
    num_blocks = token_count // GROUP
    query_blocks = query_rows.reshape(num_blocks, GROUP, head_count, head_size)
    key_blocks = key_matrix.reshape(num_blocks, GROUP, head_count, head_size)
    value_blocks = value_rows.reshape(num_blocks, GROUP, head_count, head_size)
    cumulative = jnp.cumsum(decay_log.reshape(num_blocks, GROUP, head_count), axis=1)
    block_total = cumulative[:, -1, :]
    cum_major = jnp.transpose(cumulative, (0, 2, 1))
    row_ids = lax.broadcasted_iota(jnp.int32, (GROUP, GROUP), 0)
    col_ids = lax.broadcasted_iota(jnp.int32, (GROUP, GROUP), 1)
    causal = (row_ids >= col_ids)[None, None]
    spread = cum_major[:, :, :, None] - cum_major[:, :, None, :]
    mask_weight = jnp.where(causal, jnp.exp(jnp.where(causal, spread, 0.0)), 0.0)
    scores = jnp.einsum(
        "cihd,cjhd->chij", query_blocks, key_blocks, preferred_element_type=jnp.float32
    )
    attn_weights = (scores * mask_weight).astype(jnp.bfloat16)
    local_part = jnp.einsum(
        "chij,cjhd->cihd", attn_weights, value_blocks, preferred_element_type=jnp.float32
    )

    def advance(carry_state, pieces):
        key_part, value_part, cum_part, total_part = pieces
        decayed = (key_part * jnp.exp(total_part[None, :] - cum_part)[:, :, None]).astype(
            jnp.bfloat16
        )
        fresh_term = jnp.einsum(
            "ihd,ihe->hde", decayed, value_part, preferred_element_type=jnp.float32
        )
        return (jnp.exp(total_part)[:, None, None] * carry_state + fresh_term, carry_state)

    zero_state = jnp.zeros((head_count, head_size, head_size), jnp.float32)
    end_state, local_states = lax.scan(
        advance, zero_state, (key_blocks, value_blocks, cumulative, block_total)
    )
    total_log = jnp.sum(block_total, axis=0)
    position = lax.axis_index("ctx")
    gathered, log_rates = (
        lax.all_gather(end_state[None], "ctx", axis=0, tiled=True),
        lax.all_gather(total_log[None], "ctx", axis=0, tiled=True),
    )
    incoming = weigh_gathered(gathered, log_rates, position, True)
    before = jnp.cumsum(block_total, axis=0) - block_total
    state_bf = (local_states + jnp.exp(before)[:, :, None, None] * incoming[None]).astype(
        jnp.bfloat16
    )
    carried_part = (
        jnp.einsum("cihd,chde->cihe", query_blocks, state_bf, preferred_element_type=jnp.float32)
        * jnp.exp(cumulative)[:, :, :, None]
    )
    attention = (
        (local_part + carried_part).astype(jnp.bfloat16).reshape(token_count, head_count, head_size)
    )
    attn_f = attention.astype(jnp.float32)
    grad_f = grad_out.astype(jnp.float32)
    features = head_count * lax.axis_size("head") * head_size
    square_sum = lax.psum(jnp.sum(attn_f * attn_f, axis=(1, 2)), "head")
    inv_rms = lax.rsqrt(square_sum / features + epsilon)
    output = (attn_f * inv_rms[:, None, None] * norm_gain[None]).astype(jnp.bfloat16)
    scaled_grad = norm_gain[None] * (grad_f + output.astype(jnp.float32))
    inner = lax.psum(jnp.sum(scaled_grad * attn_f, axis=(1, 2)), "head")
    grad_attention = (
        inv_rms[:, None, None] * scaled_grad
        - attn_f * (inv_rms**3 * inner / features)[:, None, None]
    ).astype(jnp.bfloat16)
    grad_blocks = grad_attention.reshape(num_blocks, GROUP, head_count, head_size)
    grad_dots = jnp.einsum(
        "cihe,cjhe->chij", grad_blocks, value_blocks, preferred_element_type=jnp.float32
    )
    grad_scores = (grad_dots * mask_weight).astype(jnp.bfloat16)
    query_local = jnp.einsum(
        "chij,cjhd->cihd", grad_scores, key_blocks, preferred_element_type=jnp.float32
    )
    key_local = jnp.einsum(
        "chij,cihd->cjhd", grad_scores, query_blocks, preferred_element_type=jnp.float32
    )
    value_local = jnp.einsum(
        "chij,cihe->cjhe", attn_weights, grad_blocks, preferred_element_type=jnp.float32
    )
    query_carried = (
        jnp.einsum("cihe,chde->cihd", grad_blocks, state_bf, preferred_element_type=jnp.float32)
        * jnp.exp(cumulative)[:, :, :, None]
    )

    def retreat(carry_state, pieces):
        query_part, grad_part, cum_part, total_part = pieces
        decayed = (query_part * jnp.exp(cum_part)[:, :, None]).astype(jnp.bfloat16)
        fresh_term = jnp.einsum(
            "ihd,ihe->hde", decayed, grad_part, preferred_element_type=jnp.float32
        )
        return (jnp.exp(total_part)[:, None, None] * carry_state + fresh_term, carry_state)

    start_state, local_back = lax.scan(
        retreat, zero_state, (query_blocks, grad_blocks, cumulative, block_total), reverse=True
    )
    gathered_back, log_back = (
        lax.all_gather(start_state[None], "ctx", axis=0, tiled=True),
        lax.all_gather(total_log[None], "ctx", axis=0, tiled=True),
    )
    arriving = weigh_gathered(gathered_back, log_back, position, False)
    after = total_log[None, :] - jnp.cumsum(block_total, axis=0)
    back_bf = (local_back + jnp.exp(after)[:, :, None, None] * arriving[None]).astype(jnp.bfloat16)
    tail = jnp.exp(block_total[:, None, :] - cumulative)[:, :, :, None]
    key_carried = (
        jnp.einsum("cihe,chde->cihd", value_blocks, back_bf, preferred_element_type=jnp.float32)
        * tail
    )
    value_carried = (
        jnp.einsum("cihd,chde->cihe", key_blocks, back_bf, preferred_element_type=jnp.float32)
        * tail
    )
    shape_out = (token_count, head_count, head_size)
    grad_query = (query_local + query_carried).astype(jnp.bfloat16).reshape(shape_out)
    grad_key = (key_local + key_carried).astype(jnp.bfloat16).reshape(shape_out)
    grad_value = (value_local + value_carried).astype(jnp.bfloat16).reshape(shape_out)
    return (output, grad_query, grad_key, grad_value)


def solution(mesh):
    placed = (
        P("ctx", "head", None),
        P("ctx", "head", None),
        P("ctx", "head", None),
        P("ctx", "head"),
        P("head", None),
        P("ctx", "head", None),
    )
    return jax.shard_map(
        per_device,
        mesh=mesh,
        in_specs=placed,
        out_specs=(
            P("ctx", "head", None),
            P("ctx", "head", None),
            P("ctx", "head", None),
            P("ctx", "head", None),
        ),
        check_vma=False,
    )
```

profile of v0, /device:TPU:1, one launch (start us, length us, event | category | flops | bytes accessed | tf_op | source)
XLA Modules:
  0.0 262.6 jit_solution(10493295506692607835)
XLA Ops:
  7.2 0.8 copy.129
  8.6 1.0 copy.79
  9.5 1.0 copy.85
  10.6 1.4 while.30
  12.0 0.6 copy-done.1
  12.9 1.3 dynamic-slice
  15.1 29.7 %all-reduce = f32[32]{0:T(128)S(1)} all-reduce(f32[32]{0:T(128)S(1)} %dynamic-update-slice), channel_id=2, replica_groups=mesh['ctx'=16,'head'=32] {'ctx'}, use_global_device_ids=true, to_apply=%add | all-reduce | flops 32 | bytes 256
  45.9 14.7 %all-gather.6.cloned.1.call-done = f32[32,128,128]{2,1,0:T(8,128)} async-done(((f32[2,128,128]{2,1,0:T(8,128)}), f32[32,128,128]{2,1,0:T(8,128)}) %all-gather.6.cloned.1.call-update) | async-done | bytes 2097168 | tf_op jit(solution)/shard_map/all_gather | solution.py:66
  60.6 3.8 %fusion.24 = f32[2,1,128,128]{3,1,2,0:T(1,128)S(1)} fusion(f32[16,2,1,1]{0,2,3,1:T(1,128)S(1)} %copy.121, f32[16,2,128,128]{3,2,1,0:T(8,128)} %bitcast.159), kind=kOutput, calls=%fused_computation.34 | convolution fusion | flops 6291456 | bytes 2228352 | tf_op jit(solution)/shard_map/nh,nhde->hde/dot_general | solution.py:24
  64.4 0.3 fusion.27
  64.6 0.3 multiply_reduce_fusion
  65.0 61.6 %psum.14 = f32[384]{0:T(512)S(1)} all-reduce(f32[384]{0:T(512)S(1)} %bitcast.171), channel_id=1, replica_groups=mesh['ctx'=16,'head'=32] {'head'}, use_global_device_ids=true, to_apply=%region_7.8 | all-reduce | flops 384 | bytes 3072 | tf_op jit(solution)/shard_map/psum | solution.py:84
  126.9 56.2 %psum.15 = f32[384]{0:T(512)S(1)} all-reduce(f32[384]{0:T(512)S(1)} %fusion.43), channel_id=1, replica_groups=mesh['ctx'=16,'head'=32] {'head'}, use_global_device_ids=true, to_apply=%region_9.10 | all-reduce | flops 384 | bytes 3072 | tf_op jit(solution)/shard_map/psum | solution.py:88
  183.4 1.2 while.31
  184.6 0.6 copy-done
  185.6 0.9 copy.117
  186.7 0.3 fusion.31
  187.3 0.9 copy.118
  188.2 60.8 %all-gather.8.cloned.1.call-done = f32[32,128,128]{2,1,0:T(8,128)} async-done(((f32[2,128,128]{2,1,0:T(8,128)}), f32[32,128,128]{2,1,0:T(8,128)}) %all-gather.8.cloned.1.call-update) | async-done | bytes 2097168 | tf_op jit(solution)/shard_map/all_gather | solution.py:124
  249.0 3.8 %fusion.22 = f32[2,1,128,128]{3,1,2,0:T(1,128)S(1)} fusion(f32[16,2,1,1]{0,2,3,1:T(1,128)S(1)} %copy.125, f32[16,2,128,128]{3,2,1,0:T(8,128)} %bitcast.160), kind=kOutput, calls=%fused_computation.32 | convolution fusion | flops 6291456 | bytes 2228352 | tf_op jit(solution)/shard_map/nh,nhde->hde/dot_general | solution.py:24
  252.8 0.3 fusion.29
  253.1 0.3 fusion.26
  253.7 0.9 copy.119
  254.9 0.9 copy.120
  (91 shorter events, 6.3 us)
Async XLA Ops:
  7.2 53.4 %all-gather.6.cloned.1.call-start = ((), (), s32[]{:S(2)}) async-start(), calls=%async_computation | async-start | bytes 2228224 | tf_op jit(solution)/shard_map/all_gather | solution.py:66
  10.6 2.3 copy-start.3
  12.0 0.7 copy-start.1
  12.6 236.4 %all-gather.8.cloned.1.call-start = ((), (), s32[]{:S(2)}) async-start(), calls=%async_computation.1 | async-start | bytes 2228224 | tf_op jit(solution)/shard_map/all_gather | solution.py:124
  64.3 62.3 %copy-start.2 = (bf16[384,2,128]{2,1,0:T(2,128)(2,1)S(1)}, bf16[384,2,128]{2,1,0:T(2,128)(2,1)}, u32[]{:S(2)}) copy-start(bf16[384,2,128]{2,1,0:T(2,128)(2,1)} %param.15) | copy-start | bytes 589828
  64.4 62.3 %copy-start.4 = (f32[2,128]{1,0:T(2,128)S(1)}, f32[2,128]{1,0:T(2,128)}, u32[]{:S(2)}) copy-start(f32[2,128]{1,0:T(2,128)} %param.14) | copy-start | bytes 3076
  184.6 0.7 copy-start
Sparse Core Ops, SparseCore 0:
  12.8 47.7 all-gather.5
  185.4 63.5 all-gather.7
where the time goes:
time: 263 us
  blocking collectives  148 us (56%)
  waiting for transfers between devices  75.5 us (29%)
  between operations  15 us (6%)
  matrix products  11.3 us (4%)
  local copies, waits for them, and re-layouts  11.2 us (4%)
    psum x1, blocking collectives, per_device(): square_sum = lax.psum(jnp.sum(attn_f * attn_f, axis=(1, 2)), 'head')  61.6 us
    all_gather x1, waiting for transfers between devices, per_device(): lax.all_gather(start_state[None], 'ctx', axis=0, tiled=True)  60.8 us
    psum x1, blocking collectives, per_device(): inner = lax.psum(jnp.sum(scaled_grad * attn_f, axis=(1, 2)), 'head')  56.2 us
    unnamed x1, blocking collectives  29.7 us
    all_gather x1, waiting for transfers between devices, per_device(): lax.all_gather(end_state[None], 'ctx', axis=0, tiled=True)  14.7 us
    unnamed x22, local copies, waits for them, and re-layouts  8.56 us
    dot_general x2, matrix products, weigh_gathered(): jnp.einsum('nh,nhde->hde', factors, gathered, precision=lax.Precision.HIG...  7.53 us
  transfers between devices with their start and end apart: 2, of which 2 were waited for; matrix products, arithmetic and copies ran while one was open for 2% of the time, Pallas kernels for 0%

commit v1 on v0

v1 whole, which is shorter than its diff:
```python
import functools

import jax
import jax.numpy as jnp
from jax import lax
from jax.experimental import pallas as pl
from jax.experimental.pallas import tpu as pltpu
from jax.sharding import PartitionSpec as P

GROUP = 128
EPSILON = 1e-06
F32 = jnp.float32
BF16 = jnp.bfloat16
MESH = pl.DeviceIdType.MESH


def dot(a, b, over):
    return lax.dot_general(a, b, (over, ((), ())), preferred_element_type=F32)


def nn(a, b):
    return dot(a, b, ((1,), (0,)))


def nt(a, b):
    return dot(a, b, ((1,), (1,)))


def tn(a, b):
    return dot(a, b, ((0,), (0,)))


def kernel(
    sizes,
    q_hbm, k_hbm, v_hbm, g_hbm, decay, gain,
    out_hbm, gq_hbm, gk_hbm, gv_hbm,
    q, k, v, g, out, gq, gk, gv,
    mask, weights, dots, attn, grad, part, value_part, key_part,
    rise, tail, fresh, states, backs, wide_k, wide_q,
    factor, ends, seen, made, came, ends2, seen2, made2, came2,
    sums, sums_x, sums2, sums_z,
    in_sem, out_sem, send_sem, recv_sem,
):
    ranks, inner_size, outer_size, blocks, features = sizes
    rows = 2 * GROUP
    pos = lax.axis_index("ctx")
    head = lax.axis_index("head")
    outer, inner = head // inner_size, head % inner_size

    order = sorted(range(1, ranks), key=lambda s: -min(s, ranks - s))
    ctx_peers = {s: lax.rem(pos + s, ranks) for s in order}
    x_peers = {s: outer * inner_size + lax.rem(inner + s, inner_size) for s in range(1, inner_size)}
    z_peers = {s: lax.rem(outer + s, outer_size) * inner_size + inner for s in range(1, outer_size)}

    barrier = pltpu.get_barrier_semaphore()
    for s in order:
        pl.semaphore_signal(barrier, 1, device_id={"ctx": ctx_peers[s]}, device_id_type=MESH)
    for peer in list(x_peers.values()) + list(z_peers.values()):
        pl.semaphore_signal(barrier, 1, device_id={"head": peer}, device_id_type=MESH)

    loads = []
    for i, (src, dst) in enumerate(((k_hbm, k), (v_hbm, v), (q_hbm, q), (g_hbm, g))):
        loads.append(pltpu.make_async_copy(src, dst, in_sem.at[i]))
        loads[-1].start()

    def send(stage, s, src, dst, where):
        copy = pltpu.make_async_remote_copy(
            src_ref=src, dst_ref=dst,
            send_sem=send_sem.at[stage, s], recv_sem=recv_sem.at[stage, s],
            device_id=where, device_id_type=MESH,
        )
        copy.start()
        return copy

    row = lax.broadcasted_iota(jnp.int32, (rows, 128), 0)
    lane = lax.broadcasted_iota(jnp.int32, (rows, 128), 1)
    even = (row % 2) == 0
    token = row // 2
    big_row = lax.broadcasted_iota(jnp.int32, (rows, rows), 0)
    big_col = lax.broadcasted_iota(jnp.int32, (rows, rows), 1)

    def block(c):
        return pl.ds(c * rows, rows)

    def wide(x):
        return jnp.concatenate(
            [jnp.where(even, x, 0.0).astype(BF16), jnp.where(even, 0.0, x).astype(BF16)], axis=1
        )

    def own_head(x):
        return jnp.where(even, x[:, :128], x[:, 128:])

    block_decay = []
    total = jnp.zeros((2, 1), F32)
    cums = []
    for c in range(blocks):
        a = decay[:, c * GROUP:(c + 1) * GROUP]
        spread = jnp.where(even, a[0:1, :], a[1:2, :])
        cum = jnp.sum(jnp.where(lane <= token, spread, 0.0), axis=1, keepdims=True)
        end = jnp.sum(a, axis=1, keepdims=True)
        total = total + end
        end_rows = jnp.where(even, end[0:1, :], end[1:2, :])
        cum_full = jnp.broadcast_to(cum, (rows, 128))
        rise[c] = jnp.exp(cum_full)
        tail[c] = jnp.exp(end_rows - cum_full)
        block_decay.append(
            jnp.exp(jnp.where(row < 128, end[0:1, :], end[1:2, :]))
        )
        cums.append(cum)
    factor[pos] = jnp.broadcast_to(jnp.exp(total), (2, 128))

    loads[0].wait()
    loads[1].wait()
    state = jnp.zeros((rows, 128), F32)
    for c in range(blocks):
        decayed = k[block(c), :].astype(F32) * tail[c]
        term = tn(wide(decayed), v[block(c), :])
        fresh[c] = term
        state = term if c == 0 else block_decay[c] * state + term
    per = rows // ranks
    ends[...] = state.reshape(ranks, per, 128)

    pl.semaphore_wait(barrier, (ranks - 1) + (inner_size - 1) + (outer_size - 1))
    copies = []

    factor_copies = [
        send(0, s, factor.at[pos], factor.at[pos], {"ctx": ctx_peers[s]}) for s in order
    ]
    copies += factor_copies

    def scatter(stage, src, dst):
        sent = [send(stage, s, src.at[ctx_peers[s]], dst.at[pos], {"ctx": ctx_peers[s]}) for s in order]
        copies.extend(sent)
        dst[pos] = src[pos]
        return sent

    def arrive(sent):
        for copy in sent:
            copy.wait_recv()

    first = scatter(1, ends, seen)

    loads[2].wait()
    loads[3].wait()
    same = (big_row % 2 == big_col % 2) & (big_row >= big_col)

    def local_forward(c):
        cum = jnp.broadcast_to(cums[c], (rows, rows))
        across = jnp.sum(jnp.where(big_row == big_col, cum, 0.0), axis=0, keepdims=True)
        m = jnp.where(same, jnp.exp(jnp.where(same, cum - across, 0.0)), 0.0)
        mask[c] = m
        w = (nt(q[block(c), :], k[block(c), :]) * m).astype(BF16)
        weights[c] = w
        part[c] = nn(w, v[block(c), :])

    half = (blocks + 1) // 2
    for c in range(half):
        local_forward(c)

    arrive(factor_copies)
    arrive(first)
    mine = pos * per < 128

    def rank_factor(n):
        f = factor[n]
        return jnp.where(mine, f[0:1, :], f[1:2, :])

    carry = jnp.zeros((per, 128), F32)
    for n in range(ranks):
        made[n] = carry
        if n + 1 < ranks:
            carry = rank_factor(n) * carry + seen[n]
    second = scatter(2, made, came)

    for c in range(half, blocks):
        local_forward(c)
    for c in range(blocks):
        wide_k[c] = wide(k[block(c), :].astype(F32))

    arrive(second)
    state = came[...].reshape(rows, 128)
    for c in range(blocks):
        if c:
            state = block_decay[c - 1] * state + fresh[c - 1]
        states[c] = state.astype(BF16)

    gain_rows = jnp.where(even, gain[0:1, :], gain[1:2, :])
    pick = token == lane

    def per_token(x):
        col = jnp.sum(x, axis=1, keepdims=True)
        return jnp.sum(jnp.where(pick, col, 0.0), axis=0, keepdims=True)

    sums[...] = jnp.zeros_like(sums)
    for c in range(blocks):
        carried = nn(wide(q[block(c), :].astype(F32)), states[c])
        a_bf = (part[c] + carried * rise[c]).astype(BF16)
        attn[c] = a_bf
        a = a_bf.astype(F32)
        ga = gain_rows * a
        sums[3 * c:3 * c + 1, :] = per_token(a * a)
        sums[3 * c + 1:3 * c + 2, :] = per_token(ga * g[block(c), :].astype(F32))
        sums[3 * c + 2:3 * c + 3, :] = per_token(ga * ga)

    x_sent = [send(3, s, sums, sums_x.at[s - 1], {"head": x_peers[s]}) for s in x_peers]
    copies += x_sent
    for c in range(blocks):
        wide_q[c] = wide(q[block(c), :].astype(F32) * rise[c])
    arrive(x_sent)
    acc = sums[...]
    for s in x_peers:
        acc = acc + sums_x[s - 1]
    sums2[...] = acc
    z_sent = [send(4, s, sums2, sums_z.at[s - 1], {"head": z_peers[s]}) for s in z_peers]
    copies += z_sent
    arrive(z_sent)
    for s in z_peers:
        acc = acc + sums_z[s - 1]

    def to_rows(x):
        return jnp.sum(jnp.where(pick, x, 0.0), axis=1, keepdims=True)

    stores = []

    def store(i, src, dst):
        copy = pltpu.make_async_copy(src, dst, out_sem.at[i])
        copy.start()
        stores.append(copy)

    for c in range(blocks):
        inv = lax.rsqrt(acc[3 * c:3 * c + 1, :] / features + EPSILON)
        total_inner = acc[3 * c + 1:3 * c + 2, :] + inv * acc[3 * c + 2:3 * c + 3, :]
        shrink = inv * inv * inv * total_inner / features
        inv_col = to_rows(inv)
        shrink_col = to_rows(shrink)
        a = attn[c].astype(F32)
        o = (a * inv_col * gain_rows).astype(BF16)
        out[block(c), :] = o
        scaled = gain_rows * (g[block(c), :].astype(F32) + o.astype(F32))
        grad[c] = (inv_col * scaled - a * shrink_col).astype(BF16)

    for c in reversed(range(blocks)):
        term = tn(wide_q[c], grad[c])
        fresh[c] = term
        state = term if c == blocks - 1 else block_decay[c] * state + term
    ends2[...] = state.reshape(ranks, per, 128)
    third = scatter(5, ends2, seen2)
    store(0, out, out_hbm)

    def local_dots(c):
        d = (nt(grad[c], v[block(c), :]) * mask[c]).astype(BF16)
        dots[c] = d
        carried = own_head(nt(grad[c], states[c]))
        gq[block(c), :] = (nn(d, k[block(c), :]) + carried * rise[c]).astype(BF16)

    def local_backward(c):
        key_part[c] = tn(dots[c], q[block(c), :])
        value_part[c] = tn(weights[c], grad[c])

    for c in range(blocks):
        local_dots(c)
    store(1, gq, gq_hbm)

    arrive(third)
    carry = jnp.zeros((per, 128), F32)
    for n in reversed(range(ranks)):
        made2[n] = carry
        if n:
            carry = rank_factor(n) * carry + seen2[n]
    fourth = scatter(6, made2, came2)
    for c in range(blocks):
        local_backward(c)

    arrive(fourth)
    state = came2[...].reshape(rows, 128)
    for c in reversed(range(blocks)):
        if c < blocks - 1:
            state = block_decay[c + 1] * state + fresh[c + 1]
        backs[c] = state.astype(BF16)
    for c in range(blocks):
        key_carried = own_head(nt(v[block(c), :], backs[c]))
        gk[block(c), :] = (key_part[c] + key_carried * tail[c]).astype(BF16)
        value_carried = nn(wide_k[c], backs[c])
        gv[block(c), :] = (value_part[c] + value_carried * tail[c]).astype(BF16)
    store(2, gk, gk_hbm)
    store(3, gv, gv_hbm)
    for copy in copies:
        copy.wait_send()
    for copy in stores:
        copy.wait()


def per_device(ranks, head_ranks, inner_size, query_rows, key_matrix, value_rows, decay_log, norm_gain, grad_out):
    tokens, heads, size = query_rows.shape
    blocks = tokens // GROUP
    rows = 2 * GROUP
    per = rows // ranks
    outer_size = head_ranks // inner_size
    flat = (tokens * heads, size)
    sizes = (ranks, inner_size, outer_size, blocks, heads * head_ranks * size)
    vm = pltpu.VMEM
    sum_rows = -(-3 * blocks // 8) * 8
    any_spec = pl.BlockSpec(memory_space=pl.ANY)
    vmem_spec = pl.BlockSpec(memory_space=pltpu.VMEM)
    state_slots = [vm((ranks, per, 128), F32)] * 4
    results = pl.pallas_call(
        functools.partial(kernel, sizes),
        out_shape=[jax.ShapeDtypeStruct(flat, BF16)] * 4,
        in_specs=[any_spec] * 4 + [vmem_spec] * 2,
        out_specs=[any_spec] * 4,
        scratch_shapes=[vm(flat, BF16)] * 8
        + [
            vm((blocks, rows, rows), F32),
            vm((blocks, rows, rows), BF16),
            vm((blocks, rows, rows), BF16),
            vm((blocks, rows, 128), BF16),
            vm((blocks, rows, 128), BF16),
            vm((blocks, rows, 128), F32),
            vm((blocks, rows, 128), F32),
            vm((blocks, rows, 128), F32),
            vm((blocks, rows, 128), F32),
            vm((blocks, rows, 128), F32),
            vm((blocks, rows, 128), F32),
            vm((blocks, rows, 128), BF16),
            vm((blocks, rows, 128), BF16),
            vm((blocks, rows, rows), BF16),
            vm((blocks, rows, rows), BF16),
            vm((ranks, 2, 128), F32),
        ]
        + state_slots
        + state_slots
        + [
            vm((sum_rows, 128), F32),
            vm((inner_size - 1, sum_rows, 128), F32),
            vm((sum_rows, 128), F32),
            vm((outer_size - 1, sum_rows, 128), F32),
            pltpu.SemaphoreType.DMA((4,)),
            pltpu.SemaphoreType.DMA((4,)),
            pltpu.SemaphoreType.DMA((7, ranks)),
            pltpu.SemaphoreType.DMA((7, ranks)),
        ],
        compiler_params=pltpu.CompilerParams(collective_id=0, has_side_effects=True),
        name="lightning",
    )(
        query_rows.reshape(flat),
        key_matrix.reshape(flat),
        value_rows.reshape(flat),
        grad_out.reshape(flat),
        decay_log.T,
        norm_gain,
    )
    return tuple(r.reshape(tokens, heads, size) for r in results)


def solution(mesh):
    ranks, head_ranks = mesh.shape["ctx"], mesh.shape["head"]
    inner_size = 4 if head_ranks % 4 == 0 and head_ranks > 4 else 1
    rows = P("ctx", "head", None)
    return jax.shard_map(
        functools.partial(per_device, ranks, head_ranks, inner_size),
        mesh=mesh,
        in_specs=(rows, rows, rows, P("ctx", "head"), P("head", None), rows),
        out_specs=(rows,) * 4,
        check_vma=False,
    )
```

time: 263 us -> 55.5 us (0.21)
  blocking collectives: 148 us -> 0 us
  waiting for transfers between devices: 75.5 us -> 0 us
  Pallas kernels: 0 us -> 50.2 us
  between operations: 15 us -> 0.65 us
  matrix products: 11.3 us -> 0 us
  local copies, waits for them, and re-layouts: 11.2 us -> 4.45 us
    psum x2 -> x0, blocking collectives: 118 us -> none  [the longest x1 61.6 us: per_device(): square_sum = lax.psum(jnp.sum(attn_f * attn_f, axis=(1, 2)), 'head')]
    all_gather x2 -> x0, waiting for transfers between devices: 75.5 us -> none  [the longest x1 60.8 us: per_device(): lax.all_gather(start_state[None], 'ctx', axis=0, tiled=True)]
    pallas_call x0 -> x1, Pallas kernels: none -> 50.2 us  [per_device(): pl.pallas_call(functools.partial(kernel, sizes), out_shape=[jax.ShapeDtyp...]
    unnamed x1 -> x0, blocking collectives: 29.7 us -> none
    dot_general x18 -> x0, matrix products: 11.3 us -> none  [the longest x2 7.53 us: weigh_gathered(): jnp.einsum('nh,nhde->hde', factors, gathered, precision=lax.Precision.HIG...]
    unnamed x22 -> x10, local copies, waits for them, and re-layouts: 8.56 us -> 4.45 us
  transfers between devices with their start and end apart: 2 -> 0, of which waited for: 2 -> 0; matrix products, arithmetic and copies ran while one was open for 2% -> 0% of each run, Pallas kernels for 0% -> 0%
where the time goes in v1:
time: 55.5 us; the launch traced here: 55.3 us
  Pallas kernels  50.2 us (90%)
  local copies, waits for them, and re-layouts  4.45 us (8%)
  between operations  0.65 us (1%)
    pallas_call x1, Pallas kernels, per_device(): pl.pallas_call(functools.partial(kernel, sizes), out_shape=[jax.ShapeDtyp...  50.2 us
    unnamed x10, local copies, waits for them, and re-layouts  4.45 us

profile of v1, /device:TPU:1, one launch (start us, length us, event | category | flops | bytes accessed | tf_op | source)
XLA Modules:
  0.0 55.3 jit_solution(1036789873036924833)
XLA Ops:
  0.6 50.2 %lightning.1 = (bf16[768,128]{1,0:T(8,128)(2,1)}, bf16[768,128]{1,0:T(8,128)(2,1)}, bf16[768,128]{1,0:T(8,128)(2,1)}, bf16[768,128]{1,0:T(8,128)(2,1)}) custom-call(bf16[768,128]{1,0:T(8,128)(2,1)} %bitcast.13, bf16[768,128]{1,0:T(8,128)(2,1)} %bitcast.14, bf16[768,128]{1,0:T(8,128)(2,1)} %bitcast.15, bf16[768,128]{1,0:T(8,128)(2,1)} %bitcast.16, ...), custom_call_target="tpu_custom_call" | custom-call | tf_op jit(solution)/shard_map/lightning/pallas_call | solution.py:306
  50.8 0.0 copy-start.2
  50.8 1.8 %copy.14 = bf16[384,2,128]{2,1,0:T(2,128)(2,1)} copy(bf16[384,2,128]{2,1,0:T(2,128)(2,1)} %bitcast.12) | data formatting | bytes 393216
  52.6 0.0 copy-done.2
  52.6 0.0 copy-start.1
  52.6 0.7 %copy.15 = bf16[384,2,128]{2,1,0:T(2,128)(2,1)} copy(bf16[384,2,128]{2,1,0:T(2,128)(2,1)S(1)} %bitcast.11) | data formatting | bytes 393216
  53.3 0.3 copy-done.1
  53.6 0.0 copy-start
  53.6 0.7 %copy.16 = bf16[384,2,128]{2,1,0:T(2,128)(2,1)} copy(bf16[384,2,128]{2,1,0:T(2,128)(2,1)S(1)} %bitcast.10) | data formatting | bytes 393216
  54.3 0.3 copy-done
  54.6 0.7 %copy.17 = bf16[384,2,128]{2,1,0:T(2,128)(2,1)} copy(bf16[384,2,128]{2,1,0:T(2,128)(2,1)S(1)} %bitcast.9) | data formatting | bytes 393216
Async XLA Ops:
  50.8 1.8 %copy-start.2 = (bf16[768,128]{1,0:T(8,128)(2,1)S(1)}, bf16[768,128]{1,0:T(8,128)(2,1)}, u32[]{:S(2)}) copy-start(bf16[768,128]{1,0:T(8,128)(2,1)} %get-tuple-element.9) | copy-start | bytes 589828
  52.6 1.0 %copy-start.1 = (bf16[768,128]{1,0:T(8,128)(2,1)S(1)}, bf16[768,128]{1,0:T(8,128)(2,1)}, u32[]{:S(2)}) copy-start(bf16[768,128]{1,0:T(8,128)(2,1)} %get-tuple-element.10) | copy-start | bytes 589828
  53.6 1.0 %copy-start = (bf16[768,128]{1,0:T(8,128)(2,1)S(1)}, bf16[768,128]{1,0:T(8,128)(2,1)}, u32[]{:S(2)}) copy-start(bf16[768,128]{1,0:T(8,128)(2,1)} %get-tuple-element.11) | copy-start | bytes 589828

commit v2 on v1

--- a/solution.py
+++ b/solution.py
@@ -32,14 +32,14 @@
 
 def kernel(
     sizes,
-    q_hbm, k_hbm, v_hbm, g_hbm, decay, gain,
-    out_hbm, gq_hbm, gk_hbm, gv_hbm,
-    q, k, v, g, out, gq, gk, gv,
+    q_hbm, k_hbm, v_hbm, g_hbm, decay_hbm, gain_hbm,
+    out, gq, gk, gv,
+    q, k, v, g, decay, gain,
     mask, weights, dots, attn, grad, part, value_part, key_part,
-    rise, tail, fresh, states, backs, wide_k, wide_q,
+    rise, tail, fresh, states, backs, wide_k, wide_q, plain_q,
     factor, ends, seen, made, came, ends2, seen2, made2, came2,
     sums, sums_x, sums2, sums_z,
-    in_sem, out_sem, send_sem, recv_sem,
+    in_sem, send_sem, recv_sem,
 ):
     ranks, inner_size, outer_size, blocks, features = sizes
     rows = 2 * GROUP
@@ -52,16 +52,17 @@
     x_peers = {s: outer * inner_size + lax.rem(inner + s, inner_size) for s in range(1, inner_size)}
     z_peers = {s: lax.rem(outer + s, outer_size) * inner_size + inner for s in range(1, outer_size)}
 
+    loads = []
+    pairs = (k_hbm, k), (v_hbm, v), (q_hbm, q), (g_hbm, g), (gain_hbm, gain), (decay_hbm, decay)
+    for i, (src, dst) in reversed(list(enumerate(pairs))):
+        loads.insert(0, pltpu.make_async_copy(src, dst, in_sem.at[i]))
+        loads[0].start()
+
     barrier = pltpu.get_barrier_semaphore()
     for s in order:
         pl.semaphore_signal(barrier, 1, device_id={"ctx": ctx_peers[s]}, device_id_type=MESH)
     for peer in list(x_peers.values()) + list(z_peers.values()):
         pl.semaphore_signal(barrier, 1, device_id={"head": peer}, device_id_type=MESH)
-
-    loads = []
-    for i, (src, dst) in enumerate(((k_hbm, k), (v_hbm, v), (q_hbm, q), (g_hbm, g))):
-        loads.append(pltpu.make_async_copy(src, dst, in_sem.at[i]))
-        loads[-1].start()
 
     def send(stage, s, src, dst, where):
         copy = pltpu.make_async_remote_copy(
@@ -90,6 +91,7 @@
     def own_head(x):
         return jnp.where(even, x[:, :128], x[:, 128:])
 
+    loads[5].wait()
     block_decay = []
     total = jnp.zeros((2, 1), F32)
     cums = []
@@ -118,7 +120,7 @@
         fresh[c] = term
         state = term if c == 0 else block_decay[c] * state + term
     per = rows // ranks
-    ends[...] = state.reshape(ranks, per, 128)
+    ends[...] = state.reshape(ranks, 2, per // 2, 128)
 
     pl.semaphore_wait(barrier, (ranks - 1) + (inner_size - 1) + (outer_size - 1))
     copies = []
@@ -128,17 +130,20 @@
     ]
     copies += factor_copies
 
-    def scatter(stage, src, dst):
-        sent = [send(stage, s, src.at[ctx_peers[s]], dst.at[pos], {"ctx": ctx_peers[s]}) for s in order]
+    def scatter(stage, half, src, dst):
+        sent = [
+            send(stage + half, s, src.at[ctx_peers[s], half], dst.at[pos, half], {"ctx": ctx_peers[s]})
+            for s in order
+        ]
         copies.extend(sent)
-        dst[pos] = src[pos]
+        dst[pos, half] = src[pos, half]
         return sent
 
     def arrive(sent):
         for copy in sent:
             copy.wait_recv()
 
-    first = scatter(1, ends, seen)
+    first = [scatter(3, half, ends, seen) for half in range(2)]
 
     loads[2].wait()
     loads[3].wait()
@@ -153,31 +158,38 @@
         weights[c] = w
         part[c] = nn(w, v[block(c), :])
 
-    half = (blocks + 1) // 2
-    for c in range(half):
+    for c in range(blocks):
         local_forward(c)
 
     arrive(factor_copies)
-    arrive(first)
     mine = pos * per < 128
 
     def rank_factor(n):
         f = factor[n]
         return jnp.where(mine, f[0:1, :], f[1:2, :])
 
-    carry = jnp.zeros((per, 128), F32)
-    for n in range(ranks):
-        made[n] = carry
-        if n + 1 < ranks:
-            carry = rank_factor(n) * carry + seen[n]
-    second = scatter(2, made, came)
-
-    for c in range(half, blocks):
-        local_forward(c)
-    for c in range(blocks):
+    def scan_ranks(steps, src, dst, half):
+        carry = jnp.zeros((per // 2, 128), F32)
+        for n in steps:
+            dst[n, half] = carry
+            if n != steps[-1]:
+                carry = rank_factor(n) * carry + src[n, half]
+
+    second = []
+    for half in range(2):
+        arrive(first[half])
+        scan_ranks(list(range(ranks)), seen, made, half)
+        second.append(scatter(5, half, made, came))
+
+    for c in range(blocks):
+        q_block = q[block(c), :].astype(F32)
         wide_k[c] = wide(k[block(c), :].astype(F32))
-
-    arrive(second)
+        wide_q[c] = wide(q_block * rise[c])
+        plain_q[c] = wide(q_block)
+
+    loads[4].wait()
+    arrive(second[0])
+    arrive(second[1])
     state = came[...].reshape(rows, 128)
     for c in range(blocks):
         if c:
@@ -191,9 +203,8 @@
         col = jnp.sum(x, axis=1, keepdims=True)
         return jnp.sum(jnp.where(pick, col, 0.0), axis=0, keepdims=True)
 
-    sums[...] = jnp.zeros_like(sums)
-    for c in range(blocks):
-        carried = nn(wide(q[block(c), :].astype(F32)), states[c])
+    for c in range(blocks):
+        carried = nn(plain_q[c], states[c])
         a_bf = (part[c] + carried * rise[c]).astype(BF16)
         attn[c] = a_bf
         a = a_bf.astype(F32)
@@ -202,16 +213,14 @@
         sums[3 * c + 1:3 * c + 2, :] = per_token(ga * g[block(c), :].astype(F32))
         sums[3 * c + 2:3 * c + 3, :] = per_token(ga * ga)
 
-    x_sent = [send(3, s, sums, sums_x.at[s - 1], {"head": x_peers[s]}) for s in x_peers]
+    x_sent = [send(1, s, sums, sums_x.at[s - 1], {"head": x_peers[s]}) for s in x_peers]
     copies += x_sent
-    for c in range(blocks):
-        wide_q[c] = wide(q[block(c), :].astype(F32) * rise[c])
     arrive(x_sent)
     acc = sums[...]
     for s in x_peers:
         acc = acc + sums_x[s - 1]
     sums2[...] = acc
-    z_sent = [send(4, s, sums2, sums_z.at[s - 1], {"head": z_peers[s]}) for s in z_peers]
+    z_sent = [send(2, s, sums2, sums_z.at[s - 1], {"head": z_peers[s]}) for s in z_peers]
     copies += z_sent
     arrive(z_sent)
     for s in z_peers:
@@ -219,13 +228,6 @@
 
     def to_rows(x):
         return jnp.sum(jnp.where(pick, x, 0.0), axis=1, keepdims=True)
-
-    stores = []
-
-    def store(i, src, dst):
-        copy = pltpu.make_async_copy(src, dst, out_sem.at[i])
-        copy.start()
-        stores.append(copy)
 
     for c in range(blocks):
         inv = lax.rsqrt(acc[3 * c:3 * c + 1, :] / features + EPSILON)
@@ -243,9 +245,8 @@
         term = tn(wide_q[c], grad[c])
         fresh[c] = term
         state = term if c == blocks - 1 else block_decay[c] * state + term
-    ends2[...] = state.reshape(ranks, per, 128)
-    third = scatter(5, ends2, seen2)
-    store(0, out, out_hbm)
+    ends2[...] = state.reshape(ranks, 2, per // 2, 128)
+    third = [scatter(7, half, ends2, seen2) for half in range(2)]
 
     def local_dots(c):
         d = (nt(grad[c], v[block(c), :]) * mask[c]).astype(BF16)
@@ -259,19 +260,17 @@
 
     for c in range(blocks):
         local_dots(c)
-    store(1, gq, gq_hbm)
-
-    arrive(third)
-    carry = jnp.zeros((per, 128), F32)
-    for n in reversed(range(ranks)):
-        made2[n] = carry
-        if n:
-            carry = rank_factor(n) * carry + seen2[n]
-    fourth = scatter(6, made2, came2)
     for c in range(blocks):
         local_backward(c)
 
-    arrive(fourth)
+    fourth = []
+    for half in range(2):
+        arrive(third[half])
+        scan_ranks(list(reversed(range(ranks))), seen2, made2, half)
+        fourth.append(scatter(9, half, made2, came2))
+
+    arrive(fourth[0])
+    arrive(fourth[1])
     state = came2[...].reshape(rows, 128)
     for c in reversed(range(blocks)):
         if c < blocks - 1:
@@ -282,11 +281,18 @@
         gk[block(c), :] = (key_part[c] + key_carried * tail[c]).astype(BF16)
         value_carried = nn(wide_k[c], backs[c])
         gv[block(c), :] = (value_part[c] + value_carried * tail[c]).astype(BF16)
-    store(2, gk, gk_hbm)
-    store(3, gv, gv_hbm)
     for copy in copies:
         copy.wait_send()
-    for copy in stores:
+
+
+def write_out(a, b, c, d, oa, ob, oc, od, sem):
+    copies = [
+        pltpu.make_async_copy(src, dst, sem.at[i])
+        for i, (src, dst) in enumerate(((a, oa), (b, ob), (c, oc), (d, od)))
+    ]
+    for copy in copies:
+        copy.start()
+    for copy in copies:
         copy.wait()
 
 
@@ -299,17 +305,19 @@
     flat = (tokens * heads, size)
     sizes = (ranks, inner_size, outer_size, blocks, heads * head_ranks * size)
     vm = pltpu.VMEM
-    sum_rows = -(-3 * blocks // 8) * 8
+    sum_rows = 3 * blocks
     any_spec = pl.BlockSpec(memory_space=pl.ANY)
     vmem_spec = pl.BlockSpec(memory_space=pltpu.VMEM)
-    state_slots = [vm((ranks, per, 128), F32)] * 4
+    state_slots = [vm((ranks, 2, per // 2, 128), F32)] * 4
     results = pl.pallas_call(
         functools.partial(kernel, sizes),
-        out_shape=[jax.ShapeDtypeStruct(flat, BF16)] * 4,
-        in_specs=[any_spec] * 4 + [vmem_spec] * 2,
-        out_specs=[any_spec] * 4,
-        scratch_shapes=[vm(flat, BF16)] * 8
+        out_shape=[pltpu.VMEM(flat, BF16)] * 4,
+        in_specs=[any_spec] * 6,
+        out_specs=[vmem_spec] * 4,
+        scratch_shapes=[vm(flat, BF16)] * 4
         + [
+            vm(decay_log.T.shape, F32),
+            vm(norm_gain.shape, F32),
             vm((blocks, rows, rows), F32),
             vm((blocks, rows, rows), BF16),
             vm((blocks, rows, rows), BF16),
@@ -323,6 +331,7 @@
             vm((blocks, rows, 128), F32),
             vm((blocks, rows, 128), BF16),
             vm((blocks, rows, 128), BF16),
+            vm((blocks, rows, rows), BF16),
             vm((blocks, rows, rows), BF16),
             vm((blocks, rows, rows), BF16),
             vm((ranks, 2, 128), F32),
@@ -334,10 +343,9 @@
             vm((inner_size - 1, sum_rows, 128), F32),
             vm((sum_rows, 128), F32),
             vm((outer_size - 1, sum_rows, 128), F32),
-            pltpu.SemaphoreType.DMA((4,)),
-            pltpu.SemaphoreType.DMA((4,)),
-            pltpu.SemaphoreType.DMA((7, ranks)),
-            pltpu.SemaphoreType.DMA((7, ranks)),
+            pltpu.SemaphoreType.DMA((6,)),
+            pltpu.SemaphoreType.DMA((11, ranks)),
+            pltpu.SemaphoreType.DMA((11, ranks)),
         ],
         compiler_params=pltpu.CompilerParams(collective_id=0, has_side_effects=True),
         name="lightning",
@@ -349,6 +357,14 @@
         decay_log.T,
         norm_gain,
     )
+    results = pl.pallas_call(
+        write_out,
+        out_shape=[jax.ShapeDtypeStruct(flat, BF16)] * 4,
+        in_specs=[vmem_spec] * 4,
+        out_specs=[any_spec] * 4,
+        scratch_shapes=[pltpu.SemaphoreType.DMA((4,))],
+        name="write_out",
+    )(*[pltpu.with_memory_space_constraint(r, pltpu.VMEM) for r in results])
     return tuple(r.reshape(tokens, heads, size) for r in results)
 
 

time: 55.5 us -> 51.5 us (0.928)
  local copies, waits for them, and re-layouts: 4.45 us -> 0 us
    unnamed x10 -> x0, local copies, waits for them, and re-layouts: 4.45 us -> none
    pallas_call x1 -> x2, Pallas kernels: 50.2 us -> 50.7 us  [the longest x1 49.8 us: per_device(): pl.pallas_call(functools.partial(kernel, sizes), out_shape=[pltpu.VMEM(fl...]
where the time goes in v2:
time: 51.5 us; the launch traced here: 51.4 us
  Pallas kernels  50.7 us (98%)
  between operations  0.64 us (1%)
    pallas_call x1, Pallas kernels, per_device(): pl.pallas_call(functools.partial(kernel, sizes), out_shape=[pltpu.VMEM(fl...  49.8 us

profile of v2, /device:TPU:1, one launch (start us, length us, event | category | flops | bytes accessed | tf_op | source)
XLA Modules:
  0.0 51.4 jit_solution(4031335511608084920)
XLA Ops:
  0.6 49.8 %lightning.1 = (bf16[768,128]{1,0:T(8,128)(2,1)S(1)}, bf16[768,128]{1,0:T(8,128)(2,1)S(1)}, bf16[768,128]{1,0:T(8,128)(2,1)S(1)}, bf16[768,128]{1,0:T(8,128)(2,1)S(1)}) custom-call(bf16[768,128]{1,0:T(8,128)(2,1)} %bitcast.9, bf16[768,128]{1,0:T(8,128)(2,1)} %bitcast.10, bf16[768,128]{1,0:T(8,128)(2,1)} %bitcast.11, bf16[768,128]{1,0:T(8,128)(2,1)} %bitcast.12, ...), custom_call_target="tpu_custom_call" | custom-call | tf_op jit(solution)/shard_map/lightning/pallas_call | solution.py:312
  50.5 0.9 %write_out.1 = (bf16[768,128]{1,0:T(8,128)(2,1)}, bf16[768,128]{1,0:T(8,128)(2,1)}, bf16[768,128]{1,0:T(8,128)(2,1)}, bf16[768,128]{1,0:T(8,128)(2,1)}) custom-call(bf16[768,128]{1,0:T(8,128)(2,1)S(1)} %get-tuple-element.12.a, bf16[768,128]{1,0:T(8,128)(2,1)S(1)} %get-tuple-element.13.b, bf16[768,128]{1,0:T(8,128)(2,1)S(1)} %get-tuple-element.14.c, ...), custom_call_target="tpu_custom_call" | custom-call | tf_op jit(solution)/shard_map/write_out/pallas_call | solution.py:360

commit v3 on v2

--- a/solution.py
+++ b/solution.py
@@ -37,7 +37,9 @@
     q, k, v, g, decay, gain,
     mask, weights, dots, attn, grad, part, value_part, key_part,
     rise, tail, fresh, states, backs, wide_k, wide_q, plain_q,
-    factor, ends, seen, made, came, ends2, seen2, made2, came2,
+    factor,
+    pack, pair_in, joined, seen, made, came, pair_out, incoming,
+    pack2, pair_in2, joined2, seen2, made2, came2, pair_out2, incoming2,
     sums, sums_x, sums2, sums_z,
     in_sem, send_sem, recv_sem,
 ):
@@ -47,8 +49,12 @@
     head = lax.axis_index("head")
     outer, inner = head // inner_size, head % inner_size
 
-    order = sorted(range(1, ranks), key=lambda s: -min(s, ranks - s))
-    ctx_peers = {s: lax.rem(pos + s, ranks) for s in order}
+    chips = ranks // 2
+    chip, core = pos // 2, pos % 2
+    partner = {"ctx": pos + 1 - 2 * core}
+    order = sorted(range(1, chips), key=lambda s: -min(s, chips - s))
+    chip_peers = {s: lax.rem(chip + s, chips) for s in order}
+    ctx_peers = {s: {"ctx": chip_peers[s] * 2 + core} for s in order}
     x_peers = {s: outer * inner_size + lax.rem(inner + s, inner_size) for s in range(1, inner_size)}
     z_peers = {s: lax.rem(outer + s, outer_size) * inner_size + inner for s in range(1, outer_size)}
 
@@ -59,8 +65,8 @@
         loads[0].start()
 
     barrier = pltpu.get_barrier_semaphore()
-    for s in order:
-        pl.semaphore_signal(barrier, 1, device_id={"ctx": ctx_peers[s]}, device_id_type=MESH)
+    for where in [ctx_peers[s] for s in order] + [partner]:
+        pl.semaphore_signal(barrier, 1, device_id=where, device_id_type=MESH)
     for peer in list(x_peers.values()) + list(z_peers.values()):
         pl.semaphore_signal(barrier, 1, device_id={"head": peer}, device_id_type=MESH)
 
@@ -109,7 +115,7 @@
             jnp.exp(jnp.where(row < 128, end[0:1, :], end[1:2, :]))
         )
         cums.append(cum)
-    factor[pos] = jnp.broadcast_to(jnp.exp(total), (2, 128))
+    own_factor = jnp.exp(total)
 
     loads[0].wait()
     loads[1].wait()
@@ -119,34 +125,60 @@
         term = tn(wide(decayed), v[block(c), :])
         fresh[c] = term
         state = term if c == 0 else block_decay[c] * state + term
-    per = rows // ranks
-    ends[...] = state.reshape(ranks, 2, per // 2, 128)
-
-    pl.semaphore_wait(barrier, (ranks - 1) + (inner_size - 1) + (outer_size - 1))
+    per = 128 // chips
+    pl.semaphore_wait(barrier, chips + (inner_size - 1) + (outer_size - 1))
     copies = []
-
-    factor_copies = [
-        send(0, s, factor.at[pos], factor.at[pos], {"ctx": ctx_peers[s]}) for s in order
-    ]
-    copies += factor_copies
-
-    def scatter(stage, half, src, dst):
-        sent = [
-            send(stage + half, s, src.at[ctx_peers[s], half], dst.at[pos, half], {"ctx": ctx_peers[s]})
-            for s in order
-        ]
-        copies.extend(sent)
-        dst[pos, half] = src[pos, half]
-        return sent
+    even_core = core == 0
 
     def arrive(sent):
         for copy in sent:
             copy.wait_recv()
 
-    first = [scatter(3, half, ends, seen) for half in range(2)]
-
-    loads[2].wait()
-    loads[3].wait()
+    def exchange(stage, state, bufs, forward, covers):
+        packed, paired, whole, held, prefix, back, passed, result = bufs
+        packed[:, :128, :] = state.reshape(2, 128, 128)
+        packed[0, 128:, :] = jnp.broadcast_to(own_factor[0:1, :], (8, 128))
+        packed[1, 128:, :] = jnp.broadcast_to(own_factor[1:2, :], (8, 128))
+        pair = send(7, stage, packed.at[1 - core], paired, partner)
+        copies.append(pair)
+        covers[0]()
+        pair.wait_recv()
+        mine, other = packed[core], paired[...]
+        low = jnp.where(even_core, mine, other)
+        high = jnp.where(even_core, other, mine)
+        low_factor, high_factor = low[128:129, :], high[128:129, :]
+        low, high = low[:128, :], high[:128, :]
+        joint = high_factor * low + high if forward else low_factor * high + low
+        whole[...] = joint.reshape(chips, per, 128)
+        held[chip] = whole[chip]
+        sent = [send(stage, s, whole.at[chip_peers[s]], held.at[chip], ctx_peers[s]) for s in order]
+        if forward:
+            factor[chip] = low_factor * high_factor
+            sent += [send(0, s, factor.at[chip], factor.at[chip], ctx_peers[s]) for s in order]
+        copies.extend(sent)
+        covers[1]()
+        arrive(sent)
+        steps = list(range(chips)) if forward else list(reversed(range(chips)))
+        carry = jnp.zeros((per, 128), F32)
+        for n in steps:
+            prefix[n] = carry
+            if n != steps[-1]:
+                carry = factor[n] * carry + held[n]
+        back[chip] = prefix[chip]
+        sent = [send(stage + 1, s, prefix.at[chip_peers[s]], back.at[chip], ctx_peers[s]) for s in order]
+        copies.extend(sent)
+        covers[2]()
+        arrive(sent)
+        first = back[...].reshape(128, 128)
+        later = low_factor * first + low if forward else high_factor * first + high
+        own_first = even_core if forward else core == 1
+        passed[...] = jnp.where(own_first, later, first)
+        pair = send(7, stage + 1, passed, result.at[core], partner)
+        copies.append(pair)
+        result[core] = jnp.where(own_first, first, later)
+        pair.wait_recv()
+        return result[...].reshape(rows, 128)
+
     same = (big_row % 2 == big_col % 2) & (big_row >= big_col)
 
     def local_forward(c):
@@ -158,39 +190,27 @@
         weights[c] = w
         part[c] = nn(w, v[block(c), :])
 
-    for c in range(blocks):
-        local_forward(c)
-
-    arrive(factor_copies)
-    mine = pos * per < 128
-
-    def rank_factor(n):
-        f = factor[n]
-        return jnp.where(mine, f[0:1, :], f[1:2, :])
-
-    def scan_ranks(steps, src, dst, half):
-        carry = jnp.zeros((per // 2, 128), F32)
-        for n in steps:
-            dst[n, half] = carry
-            if n != steps[-1]:
-                carry = rank_factor(n) * carry + src[n, half]
-
-    second = []
-    for half in range(2):
-        arrive(first[half])
-        scan_ranks(list(range(ranks)), seen, made, half)
-        second.append(scatter(5, half, made, came))
-
-    for c in range(blocks):
-        q_block = q[block(c), :].astype(F32)
-        wide_k[c] = wide(k[block(c), :].astype(F32))
-        wide_q[c] = wide(q_block * rise[c])
-        plain_q[c] = wide(q_block)
-
-    loads[4].wait()
-    arrive(second[0])
-    arrive(second[1])
-    state = came[...].reshape(rows, 128)
+    def cover_first():
+        loads[2].wait()
+        local_forward(0)
+
+    def cover_second():
+        for c in range(1, blocks):
+            local_forward(c)
+
+    def cover_third():
+        for c in range(blocks):
+            q_block = q[block(c), :].astype(F32)
+            wide_k[c] = wide(k[block(c), :].astype(F32))
+            wide_q[c] = wide(q_block * rise[c])
+            plain_q[c] = wide(q_block)
+        loads[3].wait()
+        loads[4].wait()
+
+    state = exchange(
+        3, state, (pack, pair_in, joined, seen, made, came, pair_out, incoming), True,
+        (cover_first, cover_second, cover_third),
+    )
     for c in range(blocks):
         if c:
             state = block_decay[c - 1] * state + fresh[c - 1]
@@ -245,9 +265,6 @@
         term = tn(wide_q[c], grad[c])
         fresh[c] = term
         state = term if c == blocks - 1 else block_decay[c] * state + term
-    ends2[...] = state.reshape(ranks, 2, per // 2, 128)
-    third = [scatter(7, half, ends2, seen2) for half in range(2)]
-
     def local_dots(c):
         d = (nt(grad[c], v[block(c), :]) * mask[c]).astype(BF16)
         dots[c] = d
@@ -258,20 +275,19 @@
         key_part[c] = tn(dots[c], q[block(c), :])
         value_part[c] = tn(weights[c], grad[c])
 
-    for c in range(blocks):
-        local_dots(c)
-    for c in range(blocks):
-        local_backward(c)
-
-    fourth = []
-    for half in range(2):
-        arrive(third[half])
-        scan_ranks(list(reversed(range(ranks))), seen2, made2, half)
-        fourth.append(scatter(9, half, made2, came2))
-
-    arrive(fourth[0])
-    arrive(fourth[1])
-    state = came2[...].reshape(rows, 128)
+    def back_second():
+        for c in range(1, blocks):
+            local_dots(c)
+        local_backward(0)
+
+    def back_third():
+        for c in range(1, blocks):
+            local_backward(c)
+
+    state = exchange(
+        5, state, (pack2, pair_in2, joined2, seen2, made2, came2, pair_out2, incoming2), False,
+        (lambda: local_dots(0), back_second, back_third),
+    )
     for c in reversed(range(blocks)):
         if c < blocks - 1:
             state = block_decay[c + 1] * state + fresh[c + 1]
@@ -300,7 +316,7 @@
     tokens, heads, size = query_rows.shape
     blocks = tokens // GROUP
     rows = 2 * GROUP
-    per = rows // ranks
+    chips = ranks // 2
     outer_size = head_ranks // inner_size
     flat = (tokens * heads, size)
     sizes = (ranks, inner_size, outer_size, blocks, heads * head_ranks * size)
@@ -308,7 +324,9 @@
     sum_rows = 3 * blocks
     any_spec = pl.BlockSpec(memory_space=pl.ANY)
     vmem_spec = pl.BlockSpec(memory_space=pltpu.VMEM)
-    state_slots = [vm((ranks, 2, per // 2, 128), F32)] * 4
+    state_slots = [vm((2, 136, 128), F32), vm((136, 128), F32)]
+    state_slots += [vm((chips, 128 // chips, 128), F32)] * 4
+    state_slots += [vm((128, 128), F32), vm((2, 128, 128), F32)]
     results = pl.pallas_call(
         functools.partial(kernel, sizes),
         out_shape=[pltpu.VMEM(flat, BF16)] * 4,
@@ -334,7 +352,7 @@
             vm((blocks, rows, rows), BF16),
             vm((blocks, rows, rows), BF16),
             vm((blocks, rows, rows), BF16),
-            vm((ranks, 2, 128), F32),
+            vm((chips, 1, 128), F32),
         ]
         + state_slots
         + state_slots
@@ -344,8 +362,8 @@
             vm((sum_rows, 128), F32),
             vm((outer_size - 1, sum_rows, 128), F32),
             pltpu.SemaphoreType.DMA((6,)),
-            pltpu.SemaphoreType.DMA((11, ranks)),
-            pltpu.SemaphoreType.DMA((11, ranks)),
+            pltpu.SemaphoreType.DMA((8, 8)),
+            pltpu.SemaphoreType.DMA((8, 8)),
         ],
         compiler_params=pltpu.CompilerParams(collective_id=0, has_side_effects=True),
         name="lightning",

time: 51.5 us -> 49.6 us (0.963)
  Pallas kernels: 50.7 us -> 48.8 us
    pallas_call x1, Pallas kernels: 49.8 us -> 47.9 us  [per_device(): pl.pallas_call(functools.partial(kernel, sizes), out_shape=[pltpu.VMEM(fl...]
where the time goes in v3:
time: 49.6 us; the launch traced here: 49.5 us
  Pallas kernels  48.8 us (98%)
  between operations  0.64 us (1%)
    pallas_call x1, Pallas kernels, per_device(): pl.pallas_call(functools.partial(kernel, sizes), out_shape=[pltpu.VMEM(fl...  47.9 us

profile of v3, /device:TPU:1, one launch (start us, length us, event | category | flops | bytes accessed | tf_op | source)
XLA Modules:
  0.0 49.5 jit_solution(12194716206800225842)
XLA Ops:
  0.6 47.9 %lightning.1 = (bf16[768,128]{1,0:T(8,128)(2,1)S(1)}, bf16[768,128]{1,0:T(8,128)(2,1)S(1)}, bf16[768,128]{1,0:T(8,128)(2,1)S(1)}, bf16[768,128]{1,0:T(8,128)(2,1)S(1)}) custom-call(bf16[768,128]{1,0:T(8,128)(2,1)} %bitcast.9, bf16[768,128]{1,0:T(8,128)(2,1)} %bitcast.10, bf16[768,128]{1,0:T(8,128)(2,1)} %bitcast.11, bf16[768,128]{1,0:T(8,128)(2,1)} %bitcast.12, ...), custom_call_target="tpu_custom_call" | custom-call | tf_op jit(solution)/shard_map/lightning/pallas_call | solution.py:330
  48.6 0.9 %write_out.1 = (bf16[768,128]{1,0:T(8,128)(2,1)}, bf16[768,128]{1,0:T(8,128)(2,1)}, bf16[768,128]{1,0:T(8,128)(2,1)}, bf16[768,128]{1,0:T(8,128)(2,1)}) custom-call(bf16[768,128]{1,0:T(8,128)(2,1)S(1)} %get-tuple-element.12.a, bf16[768,128]{1,0:T(8,128)(2,1)S(1)} %get-tuple-element.13.b, bf16[768,128]{1,0:T(8,128)(2,1)S(1)} %get-tuple-element.14.c, ...), custom_call_target="tpu_custom_call" | custom-call | tf_op jit(solution)/shard_map/write_out/pallas_call | solution.py:378

commit v4 on v3

--- a/solution.py
+++ b/solution.py
@@ -52,28 +52,33 @@
     chips = ranks // 2
     chip, core = pos // 2, pos % 2
     partner = {"ctx": pos + 1 - 2 * core}
-    order = sorted(range(1, chips), key=lambda s: -min(s, chips - s))
+    far_first = lambda n: sorted(range(1, n), key=lambda s: -min(s, n - s))
+    order = far_first(chips)
     chip_peers = {s: lax.rem(chip + s, chips) for s in order}
     ctx_peers = {s: {"ctx": chip_peers[s] * 2 + core} for s in order}
-    x_peers = {s: outer * inner_size + lax.rem(inner + s, inner_size) for s in range(1, inner_size)}
-    z_peers = {s: lax.rem(outer + s, outer_size) * inner_size + inner for s in range(1, outer_size)}
-
-    loads = []
+    x_peers = {s: outer * inner_size + lax.rem(inner + s, inner_size) for s in far_first(inner_size)}
+    z_peers = {s: lax.rem(outer + s, outer_size) * inner_size + inner for s in far_first(outer_size)}
+
+    loads = {}
     pairs = (k_hbm, k), (v_hbm, v), (q_hbm, q), (g_hbm, g), (gain_hbm, gain), (decay_hbm, decay)
-    for i, (src, dst) in reversed(list(enumerate(pairs))):
-        loads.insert(0, pltpu.make_async_copy(src, dst, in_sem.at[i]))
-        loads[0].start()
+    for i in (5, 0, 1, 2, 3, 4):
+        src, dst = pairs[i]
+        loads[i] = pltpu.make_async_copy(src, dst, in_sem.at[i])
+        loads[i].start()
 
     barrier = pltpu.get_barrier_semaphore()
-    for where in [ctx_peers[s] for s in order] + [partner]:
+    greet = [ctx_peers[s] for s in order]
+    greet += [{"head": peer} for peer in list(z_peers.values()) + list(x_peers.values())]
+    for where in greet + [partner]:
         pl.semaphore_signal(barrier, 1, device_id=where, device_id_type=MESH)
-    for peer in list(x_peers.values()) + list(z_peers.values()):
-        pl.semaphore_signal(barrier, 1, device_id={"head": peer}, device_id_type=MESH)
-
-    def send(stage, s, src, dst, where):
+
+    slots = iter(range(send_sem.shape[0]))
+
+    def send(src, dst, where):
+        slot = next(slots)
         copy = pltpu.make_async_remote_copy(
             src_ref=src, dst_ref=dst,
-            send_sem=send_sem.at[stage, s], recv_sem=recv_sem.at[stage, s],
+            send_sem=send_sem.at[slot], recv_sem=recv_sem.at[slot],
             device_id=where, device_id_type=MESH,
         )
         copy.start()
@@ -109,7 +114,6 @@
         total = total + end
         end_rows = jnp.where(even, end[0:1, :], end[1:2, :])
         cum_full = jnp.broadcast_to(cum, (rows, 128))
-        rise[c] = jnp.exp(cum_full)
         tail[c] = jnp.exp(end_rows - cum_full)
         block_decay.append(
             jnp.exp(jnp.where(row < 128, end[0:1, :], end[1:2, :]))
@@ -134,12 +138,12 @@
         for copy in sent:
             copy.wait_recv()
 
-    def exchange(stage, state, bufs, forward, covers):
+    def exchange(state, bufs, forward, covers):
         packed, paired, whole, held, prefix, back, passed, result = bufs
         packed[:, :128, :] = state.reshape(2, 128, 128)
         packed[0, 128:, :] = jnp.broadcast_to(own_factor[0:1, :], (8, 128))
         packed[1, 128:, :] = jnp.broadcast_to(own_factor[1:2, :], (8, 128))
-        pair = send(7, stage, packed.at[1 - core], paired, partner)
+        pair = send(packed.at[1 - core], paired, partner)
         copies.append(pair)
         covers[0]()
         pair.wait_recv()
@@ -151,10 +155,10 @@
         joint = high_factor * low + high if forward else low_factor * high + low
         whole[...] = joint.reshape(chips, per, 128)
         held[chip] = whole[chip]
-        sent = [send(stage, s, whole.at[chip_peers[s]], held.at[chip], ctx_peers[s]) for s in order]
+        sent = [send(whole.at[chip_peers[s]], held.at[chip], ctx_peers[s]) for s in order]
         if forward:
             factor[chip] = low_factor * high_factor
-            sent += [send(0, s, factor.at[chip], factor.at[chip], ctx_peers[s]) for s in order]
+            sent += [send(factor.at[chip], factor.at[chip], ctx_peers[s]) for s in order]
         copies.extend(sent)
         covers[1]()
         arrive(sent)
@@ -165,7 +169,7 @@
             if n != steps[-1]:
                 carry = factor[n] * carry + held[n]
         back[chip] = prefix[chip]
-        sent = [send(stage + 1, s, prefix.at[chip_peers[s]], back.at[chip], ctx_peers[s]) for s in order]
+        sent = [send(prefix.at[chip_peers[s]], back.at[chip], ctx_peers[s]) for s in order]
         copies.extend(sent)
         covers[2]()
         arrive(sent)
@@ -173,7 +177,7 @@
         later = low_factor * first + low if forward else high_factor * first + high
         own_first = even_core if forward else core == 1
         passed[...] = jnp.where(own_first, later, first)
-        pair = send(7, stage + 1, passed, result.at[core], partner)
+        pair = send(passed, result.at[core], partner)
         copies.append(pair)
         result[core] = jnp.where(own_first, first, later)
         pair.wait_recv()
@@ -182,6 +186,7 @@
     same = (big_row % 2 == big_col % 2) & (big_row >= big_col)
 
     def local_forward(c):
+        rise[c] = jnp.exp(jnp.broadcast_to(cums[c], (rows, 128)))
         cum = jnp.broadcast_to(cums[c], (rows, rows))
         across = jnp.sum(jnp.where(big_row == big_col, cum, 0.0), axis=0, keepdims=True)
         m = jnp.where(same, jnp.exp(jnp.where(same, cum - across, 0.0)), 0.0)
@@ -208,7 +213,7 @@
         loads[4].wait()
 
     state = exchange(
-        3, state, (pack, pair_in, joined, seen, made, came, pair_out, incoming), True,
+        state, (pack, pair_in, joined, seen, made, came, pair_out, incoming), True,
         (cover_first, cover_second, cover_third),
     )
     for c in range(blocks):
@@ -233,14 +238,14 @@
         sums[3 * c + 1:3 * c + 2, :] = per_token(ga * g[block(c), :].astype(F32))
         sums[3 * c + 2:3 * c + 3, :] = per_token(ga * ga)
 
-    x_sent = [send(1, s, sums, sums_x.at[s - 1], {"head": x_peers[s]}) for s in x_peers]
+    x_sent = [send(sums, sums_x.at[s - 1], {"head": x_peers[s]}) for s in x_peers]
     copies += x_sent
     arrive(x_sent)
     acc = sums[...]
     for s in x_peers:
         acc = acc + sums_x[s - 1]
     sums2[...] = acc
-    z_sent = [send(2, s, sums2, sums_z.at[s - 1], {"head": z_peers[s]}) for s in z_peers]
+    z_sent = [send(sums2, sums_z.at[s - 1], {"head": z_peers[s]}) for s in z_peers]
     copies += z_sent
     arrive(z_sent)
     for s in z_peers:
@@ -285,7 +290,7 @@
             local_backward(c)
 
     state = exchange(
-        5, state, (pack2, pair_in2, joined2, seen2, made2, came2, pair_out2, incoming2), False,
+        state, (pack2, pair_in2, joined2, seen2, made2, came2, pair_out2, incoming2), False,
         (lambda: local_dots(0), back_second, back_third),
     )
     for c in reversed(range(blocks)):
@@ -322,6 +327,7 @@
     sizes = (ranks, inner_size, outer_size, blocks, heads * head_ranks * size)
     vm = pltpu.VMEM
     sum_rows = 3 * blocks
+    slots = 4 + 5 * (chips - 1) + inner_size + outer_size - 2
     any_spec = pl.BlockSpec(memory_space=pl.ANY)
     vmem_spec = pl.BlockSpec(memory_space=pltpu.VMEM)
     state_slots = [vm((2, 136, 128), F32), vm((136, 128), F32)]
@@ -362,8 +368,8 @@
             vm((sum_rows, 128), F32),
             vm((outer_size - 1, sum_rows, 128), F32),
             pltpu.SemaphoreType.DMA((6,)),
-            pltpu.SemaphoreType.DMA((8, 8)),
-            pltpu.SemaphoreType.DMA((8, 8)),
+            pltpu.SemaphoreType.DMA((slots,)),
+            pltpu.SemaphoreType.DMA((slots,)),
         ],
         compiler_params=pltpu.CompilerParams(collective_id=0, has_side_effects=True),
         name="lightning",

time: 49.6 us -> 49.7 us (level)
  no operation moved by 1% of the time
where the time goes in v4:
time: 49.7 us; the launch traced here: 49.5 us
  Pallas kernels  48.9 us (98%)
  between operations  0.64 us (1%)
    pallas_call x1, Pallas kernels, per_device(): pl.pallas_call(functools.partial(kernel, sizes), out_shape=[pltpu.VMEM(fl...  48 us

profile of v4, /device:TPU:1, one launch (start us, length us, event | category | flops | bytes accessed | tf_op | source)
XLA Modules:
  0.0 49.5 jit_solution(848549982238814334)
XLA Ops:
  0.6 48.0 %lightning.1 = (bf16[768,128]{1,0:T(8,128)(2,1)S(1)}, bf16[768,128]{1,0:T(8,128)(2,1)S(1)}, bf16[768,128]{1,0:T(8,128)(2,1)S(1)}, bf16[768,128]{1,0:T(8,128)(2,1)S(1)}) custom-call(bf16[768,128]{1,0:T(8,128)(2,1)} %bitcast.9, bf16[768,128]{1,0:T(8,128)(2,1)} %bitcast.10, bf16[768,128]{1,0:T(8,128)(2,1)} %bitcast.11, bf16[768,128]{1,0:T(8,128)(2,1)} %bitcast.12, ...), custom_call_target="tpu_custom_call" | custom-call | tf_op jit(solution)/shard_map/lightning/pallas_call | solution.py:336
  48.6 0.9 %write_out.1 = (bf16[768,128]{1,0:T(8,128)(2,1)}, bf16[768,128]{1,0:T(8,128)(2,1)}, bf16[768,128]{1,0:T(8,128)(2,1)}, bf16[768,128]{1,0:T(8,128)(2,1)}) custom-call(bf16[768,128]{1,0:T(8,128)(2,1)S(1)} %get-tuple-element.12.a, bf16[768,128]{1,0:T(8,128)(2,1)S(1)} %get-tuple-element.13.b, bf16[768,128]{1,0:T(8,128)(2,1)S(1)} %get-tuple-element.14.c, ...), custom_call_target="tpu_custom_call" | custom-call | tf_op jit(solution)/shard_map/write_out/pallas_call | solution.py:384
